TPU v7x, 256 devices: a whole 4x4x8 slice. The times are simulated.
256 devices in a mesh: req: 8 (over y, core), vocab: 32 (over x, z).
Axes of the slice: x: 4, y: 4, z: 8, core: 2. Of those that a mesh axis runs over, the one named last changes fastest.
Arguments:
- hidden_rows: bfloat16 [8192, 2048], P(('req', 'vocab')), may hold values from -20 to 20
- norm_gain: float32 [2048], replicated, may hold values from 0.1 to 1.9
- head_weight: bfloat16 [2048, 81920], P(None, 'vocab'), may hold values from -10 to 10
- token_ids: int32 [8192], P('req'), may hold values from 0 to 81919
- live_count: int32 [256], P(('req', 'vocab')), may hold values from 1 to 32, as said below
Outputs:
- logprob: float32 [8192], P(('req', 'vocab'))
- entropy: float32 [8192], P(('req', 'vocab'))
Inputs may be any that keep to these rules, and one draw needn't show every extreme that they name: `live_count`: the live rows of an owner are its first ones; some owner has all 32 live in every draw.
All inputs are finite; a program needn't handle non-finite values.
Results may differ from a plain program's by a relative error of at most 0.012.
Values may be sent and summed in bfloat16 or wider, within the bound.
A program may use at most 64 MiB of HBM per device.

v0:
```python
import jax
import jax.numpy as jnp
from jax import lax
from jax.sharding import PartitionSpec as P


def local_stats(row_block, labels, columns, first_col):
    logits = jnp.dot(row_block, columns, preferred_element_type=jnp.float32)
    row_top = jnp.max(logits, axis=1)
    shifted = logits - row_top[:, None]
    powers = jnp.exp(shifted)
    row_total = jnp.sum(powers, axis=1)
    row_spread = jnp.sum(powers * shifted, axis=1)
    width = columns.shape[1]
    offset = labels - first_col
    inside = (offset >= 0) & (offset < width)
    chosen = jnp.take_along_axis(logits, jnp.clip(offset, 0, width - 1)[:, None], axis=1)[:, 0]
    row_picked = jnp.where(inside, chosen, 0.0)
    return (row_top, row_total, row_spread, row_picked)


def rescale(row_top, row_total, row_spread, global_top):
    factor = jnp.exp(row_top - global_top)
    return (row_total * factor, (row_spread + (row_top - global_top) * row_total) * factor)


def finish(global_top, row_total, row_spread, row_picked, live_count, own_rows):
    log_total = jnp.log(row_total)
    logprob = row_picked - global_top - log_total
    entropy = log_total - row_spread / row_total
    live = jnp.arange(own_rows, dtype=jnp.int32) < live_count[0]
    return (jnp.where(live, logprob, 0.0), jnp.where(live, entropy, 0.0))


def own_slice(array, start, own_rows):
    return lax.dynamic_slice_in_dim(array, start, own_rows, 0)


def per_device(hidden_rows, norm_gain, head_weight, token_ids, live_count):
    own_rows = hidden_rows.shape[0]
    shard_width = head_weight.shape[1]
    values = hidden_rows.astype(jnp.float32)
    squares = jnp.mean(values * values, axis=1)
    normed = (values * lax.rsqrt(squares + 1e-06)[:, None] * norm_gain[None, :]).astype(
        jnp.bfloat16
    )
    gathered = lax.all_gather(normed, "vocab", axis=0, tiled=True)
    first_col = lax.axis_index("vocab") * shard_width
    row_top, row_total, row_spread, row_picked = local_stats(
        gathered, token_ids, head_weight, first_col
    )
    start = lax.axis_index("vocab") * own_rows
    global_top = lax.pmax(row_top, "vocab")
    scaled_total, scaled_spread = rescale(row_top, row_total, row_spread, global_top)
    summed_total, summed_spread, summed_picked = lax.psum(
        (scaled_total, scaled_spread, row_picked), "vocab"
    )
    return finish(
        own_slice(global_top, start, own_rows),
        own_slice(summed_total, start, own_rows),
        own_slice(summed_spread, start, own_rows),
        own_slice(summed_picked, start, own_rows),
        live_count,
        own_rows,
    )


def solution(mesh):
    placed = (P(("req", "vocab"), None), P(), P(None, "vocab"), P("req"), P(("req", "vocab")))
    return jax.shard_map(
        per_device,
        mesh=mesh,
        in_specs=placed,
        out_specs=(P(("req", "vocab")), P(("req", "vocab"))),
        check_vma=False,
    )
```

profile of v0, /device:TPU:8, one launch (start us, length us, event | category | flops | bytes accessed | tf_op | source)
XLA Modules:
  0.0 353.2 jit_solution(11047198373892118158)
XLA Ops:
  7.2 0.0 all-gather.2.cloned.1.call-start
  7.2 1.0 fusion.1
  8.3 1.7 fusion.3
  9.9 0.0 all-gather.2.cloned.1.call-update
  10.6 0.7 compare_select_fusion
  11.3 83.8 %all-gather.2.cloned.1.call-done = bf16[1024,2048]{1,0:T(8,128)(2,1)} async-done(((bf16[32,2048]{1,0:T(8,128)(2,1)}), bf16[1024,2048]{1,0:T(8,128)(2,1)}) %all-gather.2.cloned.1.call-update) | async-done | bytes 4194320 | tf_op jit(solution)/shard_map/all_gather | solution.py:47
  95.2 17.6 %fusion.7 = (f32[1024]{0:T(1024)S(1)}, f32[1024,2560]{1,0:T(8,128)}) fusion(bf16[1024,2048]{1,0:T(8,128)(2,1)} %all-gather.2.cloned.1.call-done, bf16[2048,2560]{1,0:T(8,128)(2,1)} %param.7), kind=kOutput, calls=%fused_computation.22 | convolution fusion | flops 10740038656 | bytes 25169920 | tf_op jit(solution)/shard_map/dot_general | solution.py:8
  112.8 0.0 copy-start
  112.8 71.8 %pmax.7 = f32[1024]{0:T(1024)S(1)} all-reduce(f32[1024]{0:T(1024)S(1)} %get-tuple-element.11), channel_id=1, replica_groups=mesh['req'=8,'vocab'=32] {'vocab'}, use_global_device_ids=true, to_apply=%region_3.0 | all-reduce | flops 1024 | bytes 8192 | tf_op jit(solution)/shard_map/pmax | solution.py:53
  184.6 6.3 %fusion = (f32[1024]{0:T(1024)S(1)}, f32[1024]{0:T(1024)S(1)}) fusion(f32[1024,2560]{1,0:T(8,128)} %get-tuple-element.12, f32[1024]{0:T(1024)S(1)} %get-tuple-element.11), kind=kLoop, calls=%fused_computation.3 | loop fusion | flops 10483712 | bytes 10498048 | tf_op jit(solution)/shard_map/reduce_sum | solution.py:13
  190.9 17.0 %gather_fusion = f32[1024]{0:T(1024)S(1)} fusion(f32[1024,2560]{1,0:T(8,128)} %get-tuple-element.12, s32[1024]{0:T(1024)S(1)} %bitcast.8), kind=kCustom, calls=%fused_computation | custom fusion | bytes 16384 | tf_op jit(solution)/shard_map/jit(take_along_axis)/gather | solution.py:17
  208.0 0.0 copy-done
  208.0 137.7 %all-reduce = (f32[1024]{0:T(1024)S(1)}, f32[1024]{0:T(1024)S(1)}, f32[1024]{0:T(1024)S(1)}) all-reduce(f32[1024]{0:T(1024)S(1)} %select_select_fusion, f32[1024]{0:T(1024)S(1)} %get-tuple-element.8, f32[1024]{0:T(1024)S(1)} %get-tuple-element.7), channel_id=1, replica_groups=mesh['req'=8,'vocab'=32] {'vocab'}, use_global_device_ids=true, to_apply=%region_1.0 | all-reduce | flops 3072 | bytes 24576 | tf_op jit(solution)/shard_map/psum | solution.py:55
  345.8 0.6 compare_select_fusion.1
  (6 shorter events, 0.1 us)
Async XLA Ops:
  7.2 88.0 %all-gather.2.cloned.1.call-start = ((), (), s32[]{:S(2)}) async-start(), calls=%async_computation | async-start | bytes 4325376 | tf_op jit(solution)/shard_map/all_gather | solution.py:47
  112.8 95.2 %copy-start = (s32[1024]{0:T(1024)S(1)}, s32[1024]{0:T(1024)}, u32[]{:S(2)}) copy-start(s32[1024]{0:T(1024)} %param.8) | copy-start | bytes 12292
Sparse Core Ops, SparseCore 0:
  10.6 84.5 all-gather.1
where the time goes:
time: 354 us; the launch traced here: 353 us
  blocking collectives  210 us (59%)
  waiting for transfers between devices  83.9 us (24%)
  matrix products  17.6 us (5%)
  local copies, waits for them, and re-layouts  17.1 us (5%)
  between operations  14.7 us (4%)
  other arithmetic  10.4 us (3%)
    psum x1, blocking collectives, per_device(): lax.psum((scaled_total, scaled_spread, row_picked), 'vocab')  138 us
    all_gather x1, waiting for transfers between devices, per_device(): gathered = lax.all_gather(normed, 'vocab', axis=0, tiled=True)  83.8 us
    pmax x1, blocking collectives, per_device(): global_top = lax.pmax(row_top, 'vocab')  71.8 us
    dot_general x1, matrix products, local_stats(): logits = jnp.dot(row_block, columns, preferred_element_type=jnp.float32)  17.6 us
    gather x1, local copies, waits for them, and re-layouts, local_stats(): jnp.take_along_axis(logits, jnp.clip(offset, 0, width - 1)[:, None], axis=1)  17 us
  transfers between devices with their start and end apart: 1, of which 1 were waited for; matrix products, arithmetic and copies ran while one was open for 0% of the time, Pallas kernels for 0%

commit v1 on v0

--- a/solution.py
+++ b/solution.py
@@ -44,7 +44,9 @@
     normed = (values * lax.rsqrt(squares + 1e-06)[:, None] * norm_gain[None, :]).astype(
         jnp.bfloat16
     )
-    gathered = lax.all_gather(normed, "vocab", axis=0, tiled=True)
+    gathered = jnp.concatenate(
+        lax.all_to_all(jnp.stack([normed] * lax.axis_size("vocab"), 0), "vocab", 0, 0), 0
+    )
     first_col = lax.axis_index("vocab") * shard_width
     row_top, row_total, row_spread, row_picked = local_stats(
         gathered, token_ids, head_weight, first_col

time: 354 us -> 366 us (1.034)
  between operations: 14.7 us -> 1.37 us
  waiting for transfers between devices: 83.9 us -> 96.3 us
  starting transfers between devices: 0.04 us -> 11.4 us
    all_to_all x0 -> x1, waiting for transfers between devices: none -> 96.3 us  [per_device(): lax.all_to_all(jnp.stack([normed] * lax.axis_size('vocab'), 0), 'vocab',...]
    all_gather x1 -> x0, waiting for transfers between devices: 83.8 us -> none  [per_device(): gathered = lax.all_gather(normed, 'vocab', axis=0, tiled=True)]
    all_to_all x0 -> x1, starting transfers between devices: none -> 11.4 us  [per_device(): lax.all_to_all(jnp.stack([normed] * lax.axis_size('vocab'), 0), 'vocab',...]
where the time goes in v1:
time: 366 us; the launch traced here: 365 us
  blocking collectives  209 us (57%)
  waiting for transfers between devices  96.3 us (26%)
  local copies, waits for them, and re-layouts  19.5 us (5%)
  matrix products  17.6 us (5%)
  starting transfers between devices  11.4 us (3%)
  other arithmetic  9.04 us (2%)
    psum x1, blocking collectives, per_device(): lax.psum((scaled_total, scaled_spread, row_picked), 'vocab')  138 us
    all_to_all x1, waiting for transfers between devices, per_device(): lax.all_to_all(jnp.stack([normed] * lax.axis_size('vocab'), 0), 'vocab',...  96.3 us
    pmax x1, blocking collectives, per_device(): global_top = lax.pmax(row_top, 'vocab')  71.5 us
    dot_general x1, matrix products, local_stats(): logits = jnp.dot(row_block, columns, preferred_element_type=jnp.float32)  17.6 us
    gather x1, local copies, waits for them, and re-layouts, local_stats(): jnp.take_along_axis(logits, jnp.clip(offset, 0, width - 1)[:, None], axis=1)  17 us
    all_to_all x1, starting transfers between devices, per_device(): lax.all_to_all(jnp.stack([normed] * lax.axis_size('vocab'), 0), 'vocab',...  11.4 us
  transfers between devices with their start and end apart: 1, of which 1 were waited for; matrix products, arithmetic and copies ran while one was open for 0% of the time, Pallas kernels for 0%

profile of v1, /device:TPU:8, one launch (start us, length us, event | category | flops | bytes accessed | tf_op | source)
XLA Modules:
  0.0 364.7 jit_solution(8060195230436993559)
XLA Ops:
  0.6 0.0 copy-start
  0.6 1.0 fusion.1
  1.7 1.0 fusion.3
  2.7 2.5 stack.2
  5.2 11.4 %all-to-all-start = ((bf16[32,32,2048]{2,1,0:T(8,128)(2,1)}), bf16[32,32,2048]{2,1,0:T(8,128)(2,1)}, u32[]{:S(2)}, u32[]{:S(2)}) async-start(bf16[32,32,2048]{2,1,0:T(8,128)(2,1)} %stack.2), calls=%async_computation | async-start | bytes 8388608 | tf_op jit(solution)/shard_map/all_to_all | solution.py:48
  17.3 0.0 copy-done
  17.3 96.3 %all-to-all-done = bf16[32,32,2048]{2,1,0:T(8,128)(2,1)} async-done(((bf16[32,32,2048]{2,1,0:T(8,128)(2,1)}), bf16[32,32,2048]{2,1,0:T(8,128)(2,1)}, u32[]{:S(2)}, u32[]{:S(2)}) %all-to-all-start) | async-done | bytes 4194336 | tf_op jit(solution)/shard_map/all_to_all | solution.py:48
  113.6 17.6 %fusion.7 = (f32[1024]{0:T(1024)S(1)}, f32[1024,2560]{1,0:T(8,128)}) fusion(bf16[1024,2048]{1,0:T(8,128)(2,1)} %bitcast.1, bf16[2048,2560]{1,0:T(8,128)(2,1)} %param.7), kind=kOutput, calls=%fused_computation.22 | convolution fusion | flops 10740038656 | bytes 25169920 | tf_op jit(solution)/shard_map/dot_general | solution.py:8
  131.2 71.5 %pmax.7 = f32[1024]{0:T(1024)S(1)} all-reduce(f32[1024]{0:T(1024)S(1)} %get-tuple-element.11), channel_id=1, replica_groups=mesh['req'=8,'vocab'=32] {'vocab'}, use_global_device_ids=true, to_apply=%region_3.0 | all-reduce | flops 1024 | bytes 8192 | tf_op jit(solution)/shard_map/pmax | solution.py:55
  202.7 6.3 %fusion = (f32[1024]{0:T(1024)S(1)}, f32[1024]{0:T(1024)S(1)}) fusion(f32[1024,2560]{1,0:T(8,128)} %get-tuple-element.12, f32[1024]{0:T(1024)S(1)} %get-tuple-element.11), kind=kLoop, calls=%fused_computation.3 | loop fusion | flops 10483712 | bytes 10498048 | tf_op jit(solution)/shard_map/reduce_sum | solution.py:13
  209.0 17.0 %gather_fusion = f32[1024]{0:T(1024)S(1)} fusion(f32[1024,2560]{1,0:T(8,128)} %get-tuple-element.12, s32[1024]{0:T(1024)S(1)} %bitcast.9), kind=kCustom, calls=%fused_computation | custom fusion | bytes 16384 | tf_op jit(solution)/shard_map/jit(take_along_axis)/gather | solution.py:17
  226.1 138.0 %all-reduce = (f32[1024]{0:T(1024)S(1)}, f32[1024]{0:T(1024)S(1)}, f32[1024]{0:T(1024)S(1)}) all-reduce(f32[1024]{0:T(1024)S(1)} %select_select_fusion, f32[1024]{0:T(1024)S(1)} %get-tuple-element.8, f32[1024]{0:T(1024)S(1)} %get-tuple-element.7), channel_id=1, replica_groups=mesh['req'=8,'vocab'=32] {'vocab'}, use_global_device_ids=true, to_apply=%region_1.0 | all-reduce | flops 3072 | bytes 24576 | tf_op jit(solution)/shard_map/psum | solution.py:57
  364.1 0.6 compare_select_fusion.1
  (7 shorter events, 0.1 us)
Async XLA Ops:
  0.6 16.6 %copy-start = (s32[1024]{0:T(1024)S(1)}, s32[1024]{0:T(1024)}, u32[]{:S(2)}) copy-start(s32[1024]{0:T(1024)} %param.8) | copy-start | bytes 12292
  5.2 108.4 %all-to-all-start = ((bf16[32,32,2048]{2,1,0:T(8,128)(2,1)}), bf16[32,32,2048]{2,1,0:T(8,128)(2,1)}, u32[]{:S(2)}, u32[]{:S(2)}) async-start(bf16[32,32,2048]{2,1,0:T(8,128)(2,1)} %stack.2), calls=%async_computation | async-start | bytes 8388608 | tf_op jit(solution)/shard_map/all_to_all | solution.py:48
